TPU v7x, 512 devices: a whole 4x8x8 slice. The times are simulated.
512 devices in a mesh: sat: 16 (over z, core), seg: 32 (over y, x).
Axes of the slice: x: 4, y: 8, z: 8, core: 2. Of those that a mesh axis runs over, the one named last changes fastest.
Arguments:
- sens_params: bfloat16 [16, 32, 320, 1024], P('sat', 'seg'), may hold values from -0.59765625 to 0.59765625
- sens_state: bfloat16 [16, 32, 320, 64], P('sat', 'seg'), may hold values from -0.59765625 to 0.59765625
- misfit: float32 [16, 32, 320], P('sat', 'seg'), may hold values from -6 to 6
- depth: float32 [16, 32, 320], P('sat', 'seg'), may hold values from 0.2 to 0.9
- cycle_count: int32 [16, 32], P('sat', 'seg'), may hold values from 80 to 320, as said below
- node_side: int32 [16, 32, 320], P('sat', 'seg'), may hold values from 0 to 1, as said below
- transition: bfloat16 [16, 32, 64, 64], P('sat', 'seg'), may hold values from -0.75 to 0.75
- cont_sens: bfloat16 [16, 32, 64, 1024], P('sat', 'seg'), may hold values from -0.59765625 to 0.59765625
- noise_root: float32 [16, 32, 64, 64], P('sat', 'seg'), may hold values from -0.4 to 0.4
- cont_misfit: float32 [16, 32, 64], P('sat', 'seg'), may hold values from -6 to 6
Outputs:
- gram_params: float32 [1024, 1024], P('sat')
- grad_params: float32 [1024], replicated
- node_hess: float32 [16, 32, 64, 64], P('sat', 'seg')
- node_cross: float32 [16, 32, 64, 1024], P('sat', 'seg')
- node_grad: float32 [16, 32, 64], P('sat', 'seg')
- node_coupling: float32 [16, 32, 64, 64], P('sat', 'seg')
Inputs may be any that keep to these rules, and one draw needn't show every extreme that they name: `cycle_count`: in every segment some satellite has exactly 320 cycles. `node_side`: along the cycles of one satellite's segment the value never falls, and both values occur.
All inputs are finite; a program needn't handle non-finite values.
Results may differ from a plain program's by a relative error of at most 0.0015.
The roundings to bfloat16 on the way count: a program that leaves them out, or rounds other values in their place, can miss the bound.
Values sent between devices are 32-bit elements; how exact they have to be, the bound alone decides.
A program may use at most 64 MiB of HBM per device.

v0:
```python
import jax
import jax.numpy as jnp
from jax import lax
from jax.sharding import PartitionSpec as P

highest = lax.Precision.HIGHEST


def entering(value, axis, combine, identity):
    devices, position = (lax.axis_size(axis), lax.axis_index(axis))
    everything = lax.all_gather(value, axis)
    start = jnp.broadcast_to(jnp.asarray(identity, value.dtype), value.shape)

    def step(k, before):
        reached = k < position
        new = combine(before, everything[k])
        return jnp.where(reached, new, before)

    return lax.fori_loop(0, devices, step, start)


def passed_along(block, axis, distance):
    devices = range(lax.axis_size(axis))
    route = [(i - distance, i) for i in devices if i - distance in devices]
    return lax.ppermute(block, axis, route)


def add_pair(earlier, later):
    return earlier + later


def shards(
    sens_params,
    sens_state,
    misfit,
    depth,
    cycle_count,
    node_side,
    transition,
    cont_sens,
    noise_root,
    cont_misfit,
):
    sat_dev = sens_params.shape[0]
    cycles = sens_params.shape[2]
    params = sens_params.shape[3]
    states = sens_state.shape[3]
    sat_count = lax.axis_size("sat")
    seg_count = lax.axis_size("seg")
    seg_place = lax.axis_index("seg")
    positions = jnp.arange(cycles, dtype=jnp.int32)
    live_mask = (positions[None, :] < cycle_count).astype(jnp.float32)
    used_depth = live_mask * depth[:, 0]
    through = jnp.sum(used_depth, axis=1)
    prior_age = entering(through, "seg", add_pair, jnp.zeros_like(through))
    upper_tri = (positions[:, None] < positions[None, :]).astype(jnp.float32)
    inner_age = jnp.dot(used_depth, upper_tri, precision=highest)
    age_scale = 4.0 / (cycles * seg_count)
    weights = live_mask / (1.0 + (prior_age[:, None] + inner_age) * age_scale)
    root_seg = jnp.sqrt(weights)
    weighted_sens = (root_seg[:, :, None] * sens_params[:, 0]).astype(jnp.bfloat16)
    weighted_res = (root_seg * misfit[:, 0]).astype(jnp.bfloat16)
    side = node_side[:, 0].astype(jnp.float32)[:, :, None]
    state_rows = root_seg[:, :, None] * sens_state[:, 0]
    state_pair = jnp.concatenate([state_rows * (1.0 - side), state_rows * side], axis=2).astype(
        jnp.bfloat16
    )
    live_link = (seg_place < seg_count - 1).astype(jnp.float32)
    eye_block = jnp.eye(states, dtype=jnp.float32)
    root_info = (eye_block[None] + noise_root[:, 0]) * live_link
    state_map = jnp.einsum(
        "sab,sbc->sac", root_info, transition[:, 0].astype(jnp.float32), precision=highest
    )
    param_map = jnp.einsum(
        "sab,sbp->sap", root_info, cont_sens[:, 0].astype(jnp.float32), precision=highest
    ).astype(jnp.bfloat16)
    cont_res = jnp.einsum("sab,sb->sa", root_info, cont_misfit[:, 0], precision=highest).astype(
        jnp.bfloat16
    )
    stacked = jnp.concatenate([weighted_sens, param_map], axis=1).reshape(-1, params)
    res_vec = jnp.concatenate([weighted_res, -cont_res], axis=1).reshape(-1)
    norm_factor = 1.0 / (sat_dev * sat_count * seg_count)
    term = lax.dot_general(
        stacked, stacked, (((0,), (0,)), ((), ())), preferred_element_type=jnp.float32
    )
    row_block = lax.psum_scatter(
        term * norm_factor, ("sat", "seg"), scatter_dimension=0, tiled=True
    )
    gram_params = lax.all_gather(row_block, "seg", axis=0, tiled=True)
    grad_term = jnp.dot(res_vec, stacked, preferred_element_type=jnp.float32) * norm_factor
    grad_params = lax.psum(grad_term, ("sat", "seg"))
    pair_gram = jnp.einsum(
        "smi,smk->sik", state_pair, state_pair, preferred_element_type=jnp.float32
    )
    pair_cross = jnp.einsum(
        "smi,smp->sip", state_pair, weighted_sens, preferred_element_type=jnp.float32
    )
    pair_grad = jnp.einsum(
        "smi,sm->si", state_pair, weighted_res, preferred_element_type=jnp.float32
    )
    map_float = param_map.astype(jnp.float32)
    res_float = cont_res.astype(jnp.float32)
    own_hess = pair_gram[:, :states, :states] + jnp.einsum(
        "sai,saj->sij", state_map, state_map, precision=highest
    )
    own_cross = pair_cross[:, :states] + jnp.einsum(
        "sai,sap->sip", state_map, map_float, precision=highest
    )
    own_grad = pair_grad[:, :states] - jnp.einsum(
        "sai,sa->si", state_map, res_float, precision=highest
    )
    next_hess = pair_gram[:, states:, states:] + jnp.einsum(
        "sai,saj->sij", root_info, root_info, precision=highest
    )
    next_cross = pair_cross[:, states:] - jnp.einsum(
        "sai,sap->sip", root_info, map_float, precision=highest
    )
    next_grad = pair_grad[:, states:] + jnp.einsum(
        "sai,sa->si", root_info, res_float, precision=highest
    )
    coupling = -jnp.einsum("sai,saj->sij", state_map, root_info, precision=highest)
    got_hess, got_cross, got_grad = passed_along((next_hess, next_cross, next_grad), "seg", 1)
    node_hess = (own_hess + got_hess)[:, None]
    node_cross = (own_cross + got_cross)[:, None]
    node_grad = (own_grad + got_grad)[:, None]
    node_coupling = coupling[:, None]
    return (gram_params, grad_params, node_hess, node_cross, node_grad, node_coupling)


def solution(mesh):
    placed = (
        P("sat", "seg", None, None),
        P("sat", "seg", None, None),
        P("sat", "seg", None),
        P("sat", "seg", None),
        P("sat", "seg"),
        P("sat", "seg", None),
        P("sat", "seg", None, None),
        P("sat", "seg", None, None),
        P("sat", "seg", None, None),
        P("sat", "seg", None),
    )
    return jax.shard_map(
        shards,
        mesh=mesh,
        in_specs=placed,
        out_specs=(
            P("sat", None),
            P(),
            P("sat", "seg", None, None),
            P("sat", "seg", None, None),
            P("sat", "seg", None),
            P("sat", "seg", None, None),
        ),
        check_vma=False,
    )
```

profile of v0, /device:TPU:16, one launch (start us, length us, event | category | flops | bytes accessed | tf_op | source)
XLA Modules:
  0.0 479.6 jit_solution(1217586959932746977)
XLA Ops:
  7.9 1.3 fusion.38
  9.2 1.3 dynamic-slice
  10.5 1.4 dynamic-update-slice
  11.9 63.0 %all-reduce = f32[32]{0:T(128)S(1)} all-reduce(f32[32]{0:T(128)S(1)} %dynamic-update-slice), channel_id=1, replica_groups=mesh['sat'=16,'seg'=32] {'seg'}, use_global_device_ids=true, to_apply=%add | all-reduce | flops 32 | bytes 256
  74.8 40.4 %while.13 = (s32[]{:T(128)}, f32[1]{0:T(128)}, s32[]{:T(128)}, f32[32,1]{0,1:T(1,128)S(1)}, s32[]{:T(128)}) while((s32[]{:T(128)}, f32[1]{0:T(128)}, s32[]{:T(128)}, f32[32,1]{0,1:T(1,128)S(1)}, s32[]{:T(128)}) %tuple.40), condition=%wide.region_2.3_spmd, body=%wide.region_1.2_spmd.sunk | while | flops 5 | bytes 115 | solution.py:19
  76.1 0.6 constant_dynamic-slice_fusion.2
  115.2 0.7 convert_reduce_fusion
  115.9 0.7 reduce.1
  116.6 0.7 reduce.3
  117.6 1.3 fusion.1
  119.2 3.3 convolution_multiply_fusion
  122.4 0.6 copy-done.5
  123.5 3.7 collective-permute-start.2
  127.6 3.1 collective-permute-start
  131.5 4.6 collective-permute-start.1
  136.5 0.9 fusion.8
  137.3 110.4 %psum.7 = f32[1024]{0:T(1024)} all-reduce(f32[1024]{0:T(1024)S(1)} %broadcast_multiply_fusion), channel_id=1, replica_groups=mesh['sat'=16,'seg'=32] {'sat','seg'}, use_global_device_ids=true, to_apply=%region_4.5 | all-reduce | flops 1024 | bytes 8192 | tf_op jit(solution)/shard_map/psum | solution.py:91
  247.8 0.7 fusion.15
  248.4 0.9 fusion.11
  249.3 1.0 fusion.6
  250.3 171.4 %all-reduce.4.cloned.1.call-done = f32[1024,1024]{1,0:T(8,128)} async-done(((f32[1024,1024]{1,0:T(8,128)}), f32[1024,1024]{1,0:T(8,128)}) %all-reduce.4.cloned.1.call-update) | async-done | bytes 4194320
  421.8 0.8 dynamic-slice_bitcast_fusion
  422.5 49.4 %all-gather = f32[32,2,1024]{2,1,0:T(2,128)S(1)} all-gather(f32[1,2,1024]{2,1,0:T(2,128)S(1)} %dynamic-slice_bitcast_fusion), channel_id=1, replica_groups=mesh['sat'=16,'seg'=32] {'seg'}, dimensions={0}, use_global_device_ids=true | all-gather | bytes 270336 | tf_op jit(solution)/shard_map/all_gather | solution.py:89
  471.9 0.9 reshape.312
  (67 shorter events, 20.7 us)
Async XLA Ops:
  7.2 111.7 %copy-start = (bf16[1,1,64,1024]{3,2,1,0:T(8,128)(2,1)S(1)}, bf16[1,1,64,1024]{3,2,1,0:T(8,128)(2,1)}, u32[]{:S(2)}) copy-start(bf16[1,1,64,1024]{3,2,1,0:T(8,128)(2,1)} %param.19) | copy-start | bytes 393220
  7.2 111.7 %copy-start.2 = (f32[1,1,64,64]{3,2,1,0:T(8,128)S(1)}, f32[1,1,64,64]{3,2,1,0:T(8,128)}, u32[]{:S(2)}) copy-start(f32[1,1,64,64]{3,2,1,0:T(8,128)} %param.20) | copy-start | bytes 49156
  7.2 414.6 %all-reduce.4.cloned.1.call-start = ((), (), s32[]{:S(2)}) async-start(), calls=%async_computation | async-start | bytes 8388608
  122.4 0.7 copy-start.5
  122.4 0.8 copy-start.3
  122.4 8.4 %copy-start.1 = (bf16[1,1,320,1024]{3,2,1,0:T(8,128)(2,1)S(1)}, bf16[1,1,320,1024]{3,2,1,0:T(8,128)(2,1)}, u32[]{:S(2)}) copy-start(bf16[1,1,320,1024]{3,2,1,0:T(8,128)(2,1)} %param.12) | copy-start | bytes 1966084
  123.5 124.3 %collective-permute-start.2 = (f32[1,64]{1,0:T(1,128)S(1)}, f32[1,64]{1,0:T(1,128)S(1)}, u32[]{:S(2)}, u32[]{:S(2)}) collective-permute-start(f32[1,64]{1,0:T(1,128)S(1)} %convolution_add_fusion), channel_id=1, source_target_pairs={{0,1},{1,2},{2,3},{3,4},{4,5},{5,6},{6,7},{7,8},{8,9},{9,10},{10,1... | collective-permute-start | bytes 776 | tf_op jit(solution)/shard_map/ppermute | solution.py:25
  127.6 8.7 %copy-start.4 = (bf16[1,1,64,64]{3,2,1,0:T(8,128)(2,1)S(1)}, bf16[1,1,64,64]{3,2,1,0:T(8,128)(2,1)}, u32[]{:S(2)}) copy-start(bf16[1,1,64,64]{3,2,1,0:T(8,128)(2,1)} %param.18) | copy-start | bytes 24580
  127.6 120.8 %collective-permute-start = (f32[1,64,64]{2,1,0:T(8,128)S(1)}, f32[1,64,64]{2,1,0:T(8,128)S(1)}, u32[]{:S(2)}, u32[]{:S(2)}) collective-permute-start(f32[1,64,64]{2,1,0:T(8,128)S(1)} %fusion.12), channel_id=1, source_target_pairs={{0,1},{1,2},{2,3},{3,4},{4,5},{5,6},{6,7},{7,8},{8,9},{9,10},{10,1... | collective-permute-start | bytes 49160 | tf_op jit(solution)/shard_map/ppermute | solution.py:25
  131.5 117.8 %collective-permute-start.1 = (f32[1,64,1024]{2,1,0:T(8,128)S(1)}, f32[1,64,1024]{2,1,0:T(8,128)S(1)}, u32[]{:S(2)}, u32[]{:S(2)}) collective-permute-start(f32[1,64,1024]{2,1,0:T(8,128)S(1)} %fusion.7), channel_id=1, source_target_pairs={{0,1},{1,2},{2,3},{3,4},{4,5},{5,6},{6,7},{7,8},{8,9},{9,10},{10,1... | collective-permute-start | bytes 786440 | tf_op jit(solution)/shard_map/ppermute | solution.py:25
Sparse Core Ops, SparseCore 0:
  122.6 299.1 all-reduce.3
where the time goes:
time: 481 us; the launch traced here: 480 us
  blocking collectives  223 us (46%)
  waiting for transfers between devices  171 us (36%)
  local copies, waits for them, and re-layouts  23.7 us (5%)
  loops' own time  21.7 us (5%)
  between operations  14.9 us (3%)
  starting transfers between devices  11.4 us (2%)
  matrix products  9.03 us (2%)
    unnamed x2, waiting for transfers between devices  171 us
    psum x1, blocking collectives, shards(): grad_params = lax.psum(grad_term, ('sat', 'seg'))  110 us
    unnamed x1, blocking collectives  63 us
    all_gather x1, blocking collectives, shards(): gram_params = lax.all_gather(row_block, 'seg', axis=0, tiled=True)  49.4 us
    another operation x1, loops' own time, entering(): return lax.fori_loop(0, devices, step, start)  21.7 us
    dynamic_slice x32, local copies, waits for them, and re-layouts, step(): new = combine(before, everything[k])  18.7 us
    ppermute x3, starting transfers between devices, passed_along(): return lax.ppermute(block, axis, route)  11.3 us
  transfers between devices with their start and end apart: 4, of which 1 were waited for; matrix products, arithmetic and copies ran while one was open for 1% of the time, Pallas kernels for 0%

commit v1 on v0

--- a/solution.py
+++ b/solution.py
@@ -4,6 +4,9 @@
 from jax.sharding import PartitionSpec as P
 
 highest = lax.Precision.HIGHEST
+order_terms_by_axis = lambda x_part: jnp.concatenate(
+    lax.all_to_all(jnp.stack(lax.axis_size("seg") * [x_part]), "seg", 0, 0), axis=0
+)
 
 
 def entering(value, axis, combine, identity):
@@ -86,7 +89,7 @@
     row_block = lax.psum_scatter(
         term * norm_factor, ("sat", "seg"), scatter_dimension=0, tiled=True
     )
-    gram_params = lax.all_gather(row_block, "seg", axis=0, tiled=True)
+    gram_params = order_terms_by_axis(row_block)
     grad_term = jnp.dot(res_vec, stacked, preferred_element_type=jnp.float32) * norm_factor
     grad_params = lax.psum(grad_term, ("sat", "seg"))
     pair_gram = jnp.einsum(

time: 481 us -> 542 us (1.13)
  the two profiles are of different devices: /device:TPU:16 before, /device:TPU:1 now
where the time goes in v1:
time: 542 us; the launch traced here: 540 us
  waiting for transfers between devices  293 us (54%)
  blocking collectives  161 us (30%)
  local copies, waits for them, and re-layouts  24.6 us (5%)
  loops' own time  21.7 us (4%)
  between operations  14.9 us (3%)
  starting transfers between devices  10.9 us (2%)
  matrix products  9.05 us (2%)
    unnamed x2, waiting for transfers between devices  293 us
    psum x1, blocking collectives, shards(): grad_params = lax.psum(grad_term, ('sat', 'seg'))  99.3 us
    unnamed x1, blocking collectives  61.9 us
    another operation x1, loops' own time, entering(): return lax.fori_loop(0, devices, step, start)  21.7 us
    dynamic_slice x32, local copies, waits for them, and re-layouts, step(): new = combine(before, everything[k])  18.7 us
  transfers between devices with their start and end apart: 5, of which 1 were waited for; matrix products, arithmetic and copies ran while one was open for 1% of the time, Pallas kernels for 0%

profile of v1, /device:TPU:1, one launch (start us, length us, event | category | flops | bytes accessed | tf_op | source)
XLA Modules:
  0.0 540.4 jit_solution(5669127004442280263)
XLA Ops:
  7.9 1.3 fusion.38
  9.2 1.3 dynamic-slice
  10.5 1.4 dynamic-update-slice
  11.9 61.9 %all-reduce = f32[32]{0:T(128)S(1)} all-reduce(f32[32]{0:T(128)S(1)} %dynamic-update-slice), channel_id=1, replica_groups=mesh['sat'=16,'seg'=32] {'seg'}, use_global_device_ids=true, to_apply=%add | all-reduce | flops 32 | bytes 256
  73.8 40.4 %while.13 = (s32[]{:T(128)}, f32[1]{0:T(128)}, s32[]{:T(128)}, f32[32,1]{0,1:T(1,128)S(1)}, s32[]{:T(128)}) while((s32[]{:T(128)}, f32[1]{0:T(128)}, s32[]{:T(128)}, f32[32,1]{0,1:T(1,128)S(1)}, s32[]{:T(128)}) %tuple.40), condition=%wide.region_2.3_spmd, body=%wide.region_1.2_spmd.sunk | while | flops 5 | bytes 115 | solution.py:22
  114.2 0.7 convert_reduce_fusion
  114.9 0.7 reduce.1
  115.6 0.7 reduce.3
  116.5 1.3 fusion.1
  118.1 3.3 convolution_multiply_fusion
  121.4 0.8 copy-done.3
  122.6 1.3 collective-permute-start.2
  124.4 1.3 collective-permute-start
  126.4 1.3 collective-permute-start.1
  128.2 293.4 %all-reduce.4.cloned.1.call-done = f32[1024,1024]{1,0:T(8,128)} async-done(((f32[1024,1024]{1,0:T(8,128)}), f32[1024,1024]{1,0:T(8,128)}) %all-reduce.4.cloned.1.call-update) | async-done | bytes 4194320
  421.6 0.8 constant_dynamic-slice_fusion.1
  422.4 0.8 stack.2
  423.1 6.9 %all-to-all-start = ((f32[32,2,1024]{2,1,0:T(2,128)}), f32[32,2,1024]{2,1,0:T(2,128)S(1)}, u32[]{:S(2)}, u32[]{:S(2)}) async-start(f32[32,2,1024]{2,1,0:T(2,128)} %stack.2), calls=%async_computation | async-start | bytes 524288 | tf_op jit(solution)/shard_map/all_to_all | solution.py:8
  430.0 0.9 fusion.8
  430.9 99.3 %psum.7 = f32[1024]{0:T(1024)} all-reduce(f32[1024]{0:T(1024)S(1)} %broadcast_multiply_fusion), channel_id=1, replica_groups=mesh['sat'=16,'seg'=32] {'sat','seg'}, use_global_device_ids=true, to_apply=%region_4.5 | all-reduce | flops 1024 | bytes 8192 | tf_op jit(solution)/shard_map/psum | solution.py:94
  530.2 0.7 fusion.15
  530.8 0.9 fusion.11
  531.7 1.0 fusion.6
  532.7 0.9 reshape.307
  (69 shorter events, 21.3 us)
Async XLA Ops:
  7.2 110.6 %copy-start = (bf16[1,1,64,1024]{3,2,1,0:T(8,128)(2,1)S(1)}, bf16[1,1,64,1024]{3,2,1,0:T(8,128)(2,1)}, u32[]{:S(2)}) copy-start(bf16[1,1,64,1024]{3,2,1,0:T(8,128)(2,1)} %param.19) | copy-start | bytes 393220
  7.2 110.6 %copy-start.2 = (f32[1,1,64,64]{3,2,1,0:T(8,128)S(1)}, f32[1,1,64,64]{3,2,1,0:T(8,128)}, u32[]{:S(2)}) copy-start(f32[1,1,64,64]{3,2,1,0:T(8,128)} %param.20) | copy-start | bytes 49156
  7.2 414.4 %all-reduce.4.cloned.1.call-start = ((), (), s32[]{:S(2)}) async-start(), calls=%async_computation.1 | async-start | bytes 8388608
  121.3 0.8 copy-start.3
  121.3 1.0 copy-start.5
  121.3 4.3 copy-start.1
  122.6 407.6 %collective-permute-start.2 = (f32[1,64]{1,0:T(1,128)S(1)}, f32[1,64]{1,0:T(1,128)S(1)}, u32[]{:S(2)}, u32[]{:S(2)}) collective-permute-start(f32[1,64]{1,0:T(1,128)S(1)} %convolution_add_fusion), channel_id=1, source_target_pairs={{0,1},{1,2},{2,3},{3,4},{4,5},{5,6},{6,7},{7,8},{8,9},{9,10},{10,1... | collective-permute-start | bytes 776 | tf_op jit(solution)/shard_map/ppermute | solution.py:28
  124.4 3.7 copy-start.4
  124.4 406.4 %collective-permute-start = (f32[1,64,64]{2,1,0:T(8,128)S(1)}, f32[1,64,64]{2,1,0:T(8,128)S(1)}, u32[]{:S(2)}, u32[]{:S(2)}) collective-permute-start(f32[1,64,64]{2,1,0:T(8,128)S(1)} %fusion.12), channel_id=1, source_target_pairs={{0,1},{1,2},{2,3},{3,4},{4,5},{5,6},{6,7},{7,8},{8,9},{9,10},{10,1... | collective-permute-start | bytes 49160 | tf_op jit(solution)/shard_map/ppermute | solution.py:28
  126.4 405.3 %collective-permute-start.1 = (f32[1,64,1024]{2,1,0:T(8,128)S(1)}, f32[1,64,1024]{2,1,0:T(8,128)S(1)}, u32[]{:S(2)}, u32[]{:S(2)}) collective-permute-start(f32[1,64,1024]{2,1,0:T(8,128)S(1)} %fusion.7), channel_id=1, source_target_pairs={{0,1},{1,2},{2,3},{3,4},{4,5},{5,6},{6,7},{7,8},{8,9},{9,10},{10,1... | collective-permute-start | bytes 786440 | tf_op jit(solution)/shard_map/ppermute | solution.py:28
  423.1 109.6 %all-to-all-start = ((f32[32,2,1024]{2,1,0:T(2,128)}), f32[32,2,1024]{2,1,0:T(2,128)S(1)}, u32[]{:S(2)}, u32[]{:S(2)}) async-start(f32[32,2,1024]{2,1,0:T(2,128)} %stack.2), calls=%async_computation | async-start | bytes 524288 | tf_op jit(solution)/shard_map/all_to_all | solution.py:8
Sparse Core Ops, SparseCore 0:
  121.5 300.0 all-reduce.3
